TPU v7x, 32 devices: a whole 2x2x4 slice. The times are simulated.
32 devices in a mesh: dp: 4 (over y, core), row: 4 (over z), col: 2 (over x).
Axes of the slice: x: 2, y: 2, z: 4, core: 2. Of those that a mesh axis runs over, the one named last changes fastest.
Arguments:
- inputs: bfloat16 [4096, 1024], P(('dp', 'col'), 'row'), may hold values from -6 to 6
- cotangent: bfloat16 [4096, 1024], P(('dp', 'col'), 'row'), may hold values from -6 to 6
- seg_parent: int32 [52], P('dp'), may hold values from 0 to 51, as said below
- token_depth: int32 [4096], P('dp'), may hold values from 0 to 383, as said below
- ln1_gain: float32 [1024], P('row'), may hold values from 0.25 to 1.75
- ln1_bias: float32 [1024], P('row'), may hold values from -1.5 to 1.5
- w_qkv: bfloat16 [1024, 3, 1024], P('row', None, 'col'), may hold values from -0.1875 to 0.1875
- b_qv: float32 [2, 1024], P(None, 'col'), may hold values from -1.5 to 1.5
- w_out: bfloat16 [1024, 1024], P('col', 'row'), may hold values from -0.5 to 0.5
- b_out: float32 [1024], P('row'), may hold values from -1.5 to 1.5
- ln2_gain: float32 [1024], P('row'), may hold values from 0.25 to 1.75
- ln2_bias: float32 [1024], P('row'), may hold values from -1.5 to 1.5
- w_up: bfloat16 [1024, 4096], P('row', 'col'), may hold values from -0.1875 to 0.1875
- b_up: float32 [4096], P('col'), may hold values from -1.5 to 1.5
- w_down: bfloat16 [4096, 1024], P('col', 'row'), may hold values from -0.125 to 0.125
- b_down: float32 [1024], P('row'), may hold values from -1.5 to 1.5
Outputs:
- result: float32 [4096, 1024], P(('dp', 'col'), 'row')
- input_grad: float32 [4096, 1024], P(('dp', 'col'), 'row')
- grad_ln1_gain: float32 [1024], P('row')
- grad_ln1_bias: float32 [1024], P('row')
- grad_w_qkv: float32 [1024, 3, 1024], P('row', None, 'col')
- grad_b_qv: float32 [2, 1024], P(None, 'col')
- grad_w_out: float32 [1024, 1024], P('col', 'row')
- grad_b_out: float32 [1024], P('row')
- grad_ln2_gain: float32 [1024], P('row')
- grad_ln2_bias: float32 [1024], P('row')
- grad_w_up: float32 [1024, 4096], P('row', 'col')
- grad_b_up: float32 [4096], P('col')
- grad_w_down: float32 [4096, 1024], P('col', 'row')
- grad_b_down: float32 [1024], P('row')
Inputs may be any that keep to these rules, and one draw needn't show every extreme that they name: `seg_parent`: tree t holds tokens t * 1024 to (t + 1) * 1024 - 1 and segments 13 t to 13 t + 12, laid out as segment(i) says: segment 13 t is the trunk of 256 tokens and is its own parent; four of the other twelve are branches with the trunk as parent, eight are leaves, two for every branch, with that branch as parent; segment 13 t + 12 is a branch; which ids play the other parts is drawn. `token_depth`: the token at offset j of its segment has depth j in a trunk, 256 + j in a branch and 320 + j in a leaf.
All inputs are finite; a program needn't handle non-finite values.
Results may differ from a plain program's by a relative error of at most 0.011.
Values may be sent and summed in bfloat16 or wider, within the bound.
A program may use at most 192 MiB of HBM per device.

v0:
```python
import math
import jax
import jax.numpy as jnp
from jax import lax
from jax.sharding import PartitionSpec as P

HD = 128
EPS = 1e-05
MASKED = -1e30


def gelu_value(values):
    return 0.5 * values * (1.0 + jax.scipy.special.erf(values / math.sqrt(2.0)))


def gelu_slope(values):
    return 0.5 * (1.0 + jax.scipy.special.erf(values / math.sqrt(2.0))) + values * jnp.exp(
        -0.5 * values * values
    ) / math.sqrt(2.0 * math.pi)


def width_sums(first_term, second_term):
    return lax.psum((jnp.sum(first_term, axis=1), jnp.sum(second_term, axis=1)), "row")


def normalize(values, norm_gain, norm_bias, feature_count):
    row_total, square = width_sums(values, values * values)
    row_mean = row_total / feature_count
    inv_std = lax.rsqrt(square / feature_count - row_mean * row_mean + EPS)
    normed = (values - row_mean[:, None]) * inv_std[:, None]
    return (normed, inv_std, (normed * norm_gain + norm_bias).astype(jnp.bfloat16))


def normalize_back(upstream, normed, inv_std, norm_gain, feature_count):
    spread = upstream * norm_gain
    row_total, cross_sum = width_sums(spread, spread * normed)
    return inv_std[:, None] * (
        spread - row_total[:, None] / feature_count - normed * (cross_sum[:, None] / feature_count)
    )


def contract(left_op, right_op, flipped):
    if flipped:
        return lax.dot_general(
            left_op, right_op, (((1,), (1,)), ((), ())), preferred_element_type=jnp.float32
        )
    return jnp.dot(left_op, right_op, preferred_element_type=jnp.float32)


def outer_sum(left_op, right_op):
    return lax.dot_general(
        left_op, right_op, (((0,), (0,)), ((), ())), preferred_element_type=jnp.float32
    )


def across_rows(operand, weight_block, flipped):
    gathered = lax.all_gather(operand, "col", axis=0, tiled=True)
    row_count = gathered.shape[0] // lax.axis_size("row")

    def partial_term(row_start, row_num):
        return contract(gathered, weight_block, flipped)

    return (
        lax.psum_scatter(
            partial_term(jnp.int32(0), row_count * lax.axis_size("row")),
            "row",
            scatter_dimension=0,
            tiled=True,
        ),
        gathered,
    )


def across_cols(operand, weight_block, flipped):
    gathered = lax.all_gather(operand, "row", axis=0, tiled=True)
    row_count = gathered.shape[0] // lax.axis_size("col")

    def partial_term(row_start, row_num):
        return contract(gathered, weight_block, flipped)

    return (
        lax.psum_scatter(
            partial_term(jnp.int32(0), row_count * lax.axis_size("col")),
            "col",
            scatter_dimension=0,
            tiled=True,
        ),
        gathered,
    )


def tree_labels(seg_parent, token_depth):
    seg_count = seg_parent.shape[0]
    tree_len = token_depth.shape[0]
    seg_len = tree_len // 16
    slot_ids = jnp.arange(seg_count, dtype=jnp.int32)
    where_at = jnp.arange(tree_len, dtype=jnp.int32)
    segment = jnp.where(where_at < 4 * seg_len, 0, 1 + (where_at - 4 * seg_len) // seg_len)
    parent_local = seg_parent - lax.axis_index("dp") * seg_count
    parent_one = jnp.sum(
        jnp.where(segment[:, None] == slot_ids[None, :], parent_local[None, :], 0), axis=1
    )
    parent_two = jnp.sum(
        jnp.where(parent_one[:, None] == slot_ids[None, :], parent_local[None, :], 0), axis=1
    )
    return (segment, parent_one, parent_two, token_depth)


def block_scores(query_block, key_rows, labels, query_start, slopes):
    segment, parent_one, parent_two, token_depth = labels
    block_size = query_block.shape[0]
    query_seg = lax.dynamic_slice_in_dim(segment, query_start, block_size, 0)
    query_one = lax.dynamic_slice_in_dim(parent_one, query_start, block_size, 0)
    query_two = lax.dynamic_slice_in_dim(parent_two, query_start, block_size, 0)
    query_depth = lax.dynamic_slice_in_dim(token_depth, query_start, block_size, 0)
    allowed = (
        (segment[None, :] == query_seg[:, None])
        | (segment[None, :] == query_one[:, None])
        | (segment[None, :] == query_two[:, None])
    ) & (token_depth[None, :] <= query_depth[:, None])
    score_scale = query_block.shape[2] ** (-0.5)
    raw = jnp.einsum("qhd,khd->hqk", query_block, key_rows, preferred_element_type=jnp.float32)
    distance = (query_depth[:, None] - token_depth[None, :]).astype(jnp.float32)
    scores = raw * score_scale - slopes[:, None, None] * distance[None]
    return jnp.where(allowed[None], scores, MASKED)


def attention_forward(queries, key_rows, value_rows, labels, slopes, offset):
    block_size = min(512, queries.shape[0])
    blocks = queries.shape[0] // block_size

    def one_block(block_index):
        block_first = block_index * block_size
        query_block = lax.dynamic_slice_in_dim(queries, block_first, block_size, 0)
        scores = block_scores(query_block, key_rows, labels, offset + block_first, slopes)
        top_score = jnp.max(scores, axis=2, keepdims=True)
        weights = jnp.exp(scores - top_score)
        weight_total = jnp.sum(weights, axis=2, keepdims=True)
        probs = (weights / weight_total).astype(jnp.bfloat16)
        mixed = jnp.einsum("hqk,khd->qhd", probs, value_rows, preferred_element_type=jnp.float32)
        return (mixed, (top_score + jnp.log(weight_total))[:, :, 0])

    return lax.map(one_block, jnp.arange(blocks, dtype=jnp.int32))


def attention_backward(
    queries, key_rows, value_rows, grad_mixed, log_total, labels, slopes, offset
):
    block_size = min(512, queries.shape[0])
    blocks = queries.shape[0] // block_size
    score_scale = queries.shape[2] ** (-0.5)

    def one_block(carry, items):
        key_grad, value_grad = carry
        block_index, block_total = items
        block_first = block_index * block_size
        query_block = lax.dynamic_slice_in_dim(queries, block_first, block_size, 0)
        grad_block = lax.dynamic_slice_in_dim(grad_mixed, block_first, block_size, 0)
        scores = block_scores(query_block, key_rows, labels, offset + block_first, slopes)
        probs = jnp.exp(scores - block_total[:, :, None])
        grad_probs = jnp.einsum(
            "qhd,khd->hqk", grad_block, value_rows, preferred_element_type=jnp.float32
        )
        centre = jnp.sum(probs * grad_probs, axis=2, keepdims=True)
        grad_scores = (probs * (grad_probs - centre)).astype(jnp.bfloat16)
        query_grad = (
            jnp.einsum("hqk,khd->qhd", grad_scores, key_rows, preferred_element_type=jnp.float32)
            * score_scale
        )
        key_grad = (
            key_grad
            + jnp.einsum(
                "hqk,qhd->khd", grad_scores, query_block, preferred_element_type=jnp.float32
            )
            * score_scale
        )
        value_grad = value_grad + jnp.einsum(
            "hqk,qhd->khd",
            probs.astype(jnp.bfloat16),
            grad_block,
            preferred_element_type=jnp.float32,
        )
        return ((key_grad, value_grad), query_grad)

    empty = jnp.zeros(key_rows.shape, jnp.float32)
    (key_grad, value_grad), query_grad = lax.scan(
        one_block, (empty, empty), (jnp.arange(blocks, dtype=jnp.int32), log_total)
    )
    return (key_grad, value_grad, query_grad)


def on_device(
    inputs,
    cotangent,
    seg_parent,
    token_depth,
    ln1_gain,
    ln1_bias,
    w_qkv,
    b_qv,
    w_out,
    b_out,
    ln2_gain,
    ln2_bias,
    w_up,
    b_up,
    w_down,
    b_down,
):
    feature_count = inputs.shape[1] * lax.axis_size("row")
    col_width = w_qkv.shape[2]
    heads_here = col_width // HD
    qkv_flat = w_qkv.reshape(w_qkv.shape[0], 3 * col_width)
    labels = tree_labels(seg_parent, token_depth)
    heads_seen = lax.axis_index("col") * heads_here + jnp.arange(heads_here, dtype=jnp.int32)
    slopes = jnp.exp2(-(heads_seen + 1).astype(jnp.float32))
    states = inputs.astype(jnp.float32)
    normed_one, inv_one, entry_one = normalize(states, ln1_gain, ln1_bias, feature_count)
    projected, entry_one_all = across_rows(entry_one, qkv_flat, False)
    tok_rows = projected.shape[0]
    projected = projected.reshape(tok_rows, 3, col_width)
    queries = (projected[:, 0] + b_qv[0]).astype(jnp.bfloat16)
    keys_here = projected[:, 1].astype(jnp.bfloat16)
    values_here = (projected[:, 2] + b_qv[1]).astype(jnp.bfloat16)
    pair_all = lax.all_gather(
        jnp.stack([keys_here, values_here], axis=1), "row", axis=0, tiled=True
    )
    key_rows = pair_all[:, 0].reshape(-1, heads_here, HD)
    value_rows = pair_all[:, 1].reshape(-1, heads_here, HD)
    query_heads = queries.reshape(tok_rows, heads_here, HD)
    offset = lax.axis_index("row") * tok_rows
    mixed, log_total = attention_forward(query_heads, key_rows, value_rows, labels, slopes, offset)
    mixed = mixed.reshape(tok_rows, col_width).astype(jnp.bfloat16)
    attn_out, mixed_all = across_cols(mixed, w_out, False)
    middle = states + attn_out + b_out
    normed_two, inv_two, entry_two = normalize(middle, ln2_gain, ln2_bias, feature_count)
    hidden_pre, entry_two_all = across_rows(entry_two, w_up, False)
    hidden_pre = hidden_pre + b_up
    hidden = gelu_value(hidden_pre).astype(jnp.bfloat16)
    ffn_out, hidden_all = across_cols(hidden, w_down, False)
    result = middle + ffn_out + b_down
    grad_hidden, down_all = across_rows(cotangent, w_down, True)
    grad_pre = (grad_hidden * gelu_slope(hidden_pre)).astype(jnp.bfloat16)
    grad_entry_two, pre_all = across_cols(grad_pre, w_up, True)
    grad_middle = cotangent.astype(jnp.float32) + normalize_back(
        grad_entry_two, normed_two, inv_two, ln2_gain, feature_count
    )
    grad_branch = grad_middle.astype(jnp.bfloat16)
    grad_mixed, branch_all = across_rows(grad_branch, w_out, True)
    grad_mixed = grad_mixed.astype(jnp.bfloat16).reshape(tok_rows, heads_here, HD)
    key_grad, value_grad, query_grad = attention_backward(
        query_heads, key_rows, value_rows, grad_mixed, log_total, labels, slopes, offset
    )
    kv_grads = lax.psum_scatter(
        jnp.stack([key_grad.reshape(-1, col_width), value_grad.reshape(-1, col_width)], axis=1),
        "row",
        scatter_dimension=0,
        tiled=True,
    )
    grad_projected = jnp.stack(
        [
            query_grad.reshape(tok_rows, col_width).astype(jnp.bfloat16),
            kv_grads[:, 0].astype(jnp.bfloat16),
            kv_grads[:, 1].astype(jnp.bfloat16),
        ],
        axis=1,
    )
    grad_entry_one, proj_all = across_cols(
        grad_projected.reshape(tok_rows, 3 * col_width), qkv_flat, True
    )
    input_grad = grad_middle + normalize_back(
        grad_entry_one, normed_one, inv_one, ln1_gain, feature_count
    )
    proj_sums = jnp.sum(proj_all.astype(jnp.float32), axis=0).reshape(3, col_width)
    weight_terms = (
        outer_sum(entry_one_all, proj_all).reshape(w_qkv.shape),
        jnp.stack([proj_sums[0], proj_sums[2]], axis=0),
        outer_sum(mixed_all, branch_all),
        jnp.sum(branch_all.astype(jnp.float32), axis=0),
        outer_sum(entry_two_all, pre_all),
        jnp.sum(pre_all.astype(jnp.float32), axis=0),
        outer_sum(hidden_all, down_all),
        jnp.sum(down_all.astype(jnp.float32), axis=0),
    )
    (
        grad_w_qkv,
        grad_b_qv,
        grad_w_out,
        grad_b_out,
        grad_w_up,
        grad_b_up,
        grad_w_down,
        grad_b_down,
    ) = lax.psum(
        (
            weight_terms[0],
            weight_terms[1],
            weight_terms[2],
            weight_terms[3],
            weight_terms[4],
            weight_terms[5],
            weight_terms[6],
            weight_terms[7],
        ),
        "dp",
    )
    norm_terms = (
        jnp.sum(grad_entry_one * normed_one, axis=0),
        jnp.sum(grad_entry_one, axis=0),
        jnp.sum(grad_entry_two * normed_two, axis=0),
        jnp.sum(grad_entry_two, axis=0),
    )
    grad_ln1_gain, grad_ln1_bias, grad_ln2_gain, grad_ln2_bias = lax.psum(
        (norm_terms[0], norm_terms[1], norm_terms[2], norm_terms[3]), ("dp", "col")
    )
    return (
        result,
        input_grad,
        grad_ln1_gain,
        grad_ln1_bias,
        grad_w_qkv,
        grad_b_qv,
        grad_w_out,
        grad_b_out,
        grad_ln2_gain,
        grad_ln2_bias,
        grad_w_up,
        grad_b_up,
        grad_w_down,
        grad_b_down,
    )


def solution(mesh):
    placed = (
        P(("dp", "col"), "row"),
        P(("dp", "col"), "row"),
        P("dp"),
        P("dp"),
        P("row"),
        P("row"),
        P("row", None, "col"),
        P(None, "col"),
        P("col", "row"),
        P("row"),
        P("row"),
        P("row"),
        P("row", "col"),
        P("col"),
        P("col", "row"),
        P("row"),
    )
    return jax.shard_map(
        on_device,
        mesh=mesh,
        in_specs=placed,
        out_specs=(
            P(("dp", "col"), "row"),
            P(("dp", "col"), "row"),
            P("row"),
            P("row"),
            P("row", None, "col"),
            P(None, "col"),
            P("col", "row"),
            P("row"),
            P("row"),
            P("row"),
            P("row", "col"),
            P("col"),
            P("col", "row"),
            P("row"),
        ),
        check_vma=False,
    )
```

profile of v0, /device:TPU:0, one launch (start us, length us, event | category | flops | bytes accessed | tf_op | source)
XLA Modules:
  0.0 1127.7 jit_solution(2528115706905828047)
XLA Ops:
  8.5 13.5 %all-reduce.4 = (f32[512]{0:T(512)S(1)}, f32[512]{0:T(512)S(1)}) all-reduce(f32[512]{0:T(512)S(1)} %get-tuple-element.134, f32[512]{0:T(512)S(1)} %get-tuple-element.133), channel_id=1, replica_groups=mesh['dp'=4,'row'=4,'col'=2] {'row'}, use_global_device_ids=true, to_apply=%region_3.4 | all-reduce | flops 1024 | bytes 8192 | tf_op jit(solution)/shard_map/psum | solution.py:23
  23.1 7.0 all_gather.27
  31.8 3.7 fusion.46
  36.2 108.4 %reduce-scatter.10.cloned.1.call-done = f32[256,1536]{1,0:T(8,128)} async-done(((f32[1024,1536]{1,0:T(8,128)}), f32[256,1536]{1,0:T(8,128)}) %reduce-scatter.10.cloned.1.call-update) | async-done | bytes 1572880 | tf_op jit(solution)/shard_map/reduce_scatter | solution.py:64
  144.6 1.9 copy.48
  149.7 44.8 %all-gather.6.cloned.1.call-done = bf16[1024,2,512]{0,2,1:T(8,128)(2,1)} async-done(((bf16[256,2,512]{0,2,1:T(8,128)(2,1)}), bf16[1024,2,512]{0,2,1:T(8,128)(2,1)}) %all-gather.6.cloned.1.call-update) | async-done | bytes 2097168 | tf_op jit(solution)/shard_map/all_gather | solution.py:225
  194.5 1.8 fusion.41
  196.4 1.8 fusion.45
  199.2 1.9 fusion.13
  201.1 28.5 %all-gather.8.cloned.1.call-done = bf16[1024,512]{0,1:T(8,128)(2,1)} async-done(((bf16[256,512]{0,1:T(8,128)(2,1)}), bf16[1024,512]{0,1:T(8,128)(2,1)}) %all-gather.8.cloned.1.call-update) | async-done | bytes 1048592 | tf_op jit(solution)/shard_map/all_gather | solution.py:75
  229.7 2.7 fusion.47
  232.4 10.4 all_gather.32
  243.6 5.8 fusion.50
  249.5 2.9 reduce-scatter.12.cloned.1.call-done
  253.7 10.6 all-reduce.3
  264.5 7.0 all_gather.30
  272.3 4.5 fusion.48
  276.9 121.6 %reduce-scatter.18.cloned.1.call-done = f32[256,2048]{1,0:T(8,128)} async-done(((f32[1024,2048]{1,0:T(8,128)}), f32[256,2048]{1,0:T(8,128)}) %reduce-scatter.18.cloned.1.call-update) | async-done | bytes 2097168 | tf_op jit(solution)/shard_map/reduce_scatter | solution.py:64
  398.5 147.5 %reduce-scatter.14.cloned.1.call-done = f32[256,2048]{1,0:T(8,128)} async-done(((f32[1024,2048]{1,0:T(8,128)}), f32[256,2048]{1,0:T(8,128)}) %reduce-scatter.14.cloned.1.call-update) | async-done | bytes 2097168 | tf_op jit(solution)/shard_map/reduce_scatter | solution.py:64
  546.0 3.7 fusion.7
  550.7 80.7 %all-gather.12.cloned.1.call-done = bf16[1024,2048]{1,0:T(8,128)(2,1)} async-done(((bf16[256,2048]{1,0:T(8,128)(2,1)}), bf16[1024,2048]{1,0:T(8,128)(2,1)}) %all-gather.12.cloned.1.call-update) | async-done | bytes 4194320 | tf_op jit(solution)/shard_map/all_gather | solution.py:75
  631.3 4.4 fusion.51
  635.9 77.0 %all-gather.10.cloned.1.call-done = bf16[1024,2048]{1,0:T(8,128)(2,1)} async-done(((bf16[256,2048]{1,0:T(8,128)(2,1)}), bf16[1024,2048]{1,0:T(8,128)(2,1)}) %all-gather.10.cloned.1.call-update) | async-done | bytes 4194320 | tf_op jit(solution)/shard_map/all_gather | solution.py:75
  712.9 4.7 fusion.49
  717.7 17.0 %reduce-scatter.20.cloned.1.call-done = f32[512,256]{1,0:T(8,128)} async-done(((f32[1024,256]{1,0:T(8,128)}), f32[512,256]{1,0:T(8,128)}) %reduce-scatter.20.cloned.1.call-update) | async-done | bytes 524304 | tf_op jit(solution)/shard_map/reduce_scatter | solution.py:82
  736.1 11.7 %all-reduce.2 = (f32[512]{0:T(512)S(1)}, f32[512]{0:T(512)S(1)}) all-reduce(f32[512]{0:T(512)S(1)} %get-tuple-element.124, f32[512]{0:T(512)S(1)} %get-tuple-element.128), channel_id=1, replica_groups=mesh['dp'=4,'row'=4,'col'=2] {'row'}, use_global_device_ids=true, to_apply=%region_21.22 | all-reduce | flops 1024 | bytes 8192 | tf_op jit(solution)/shard_map/psum | solution.py:23
  747.8 9.9 reduce-scatter.16.cloned.1.call-done
  757.7 2.4 fusion.39
  760.1 8.7 all_gather.34
  768.8 1.8 fusion.52
  770.7 44.0 %reduce-scatter.22.cloned.1.call-done = f32[256,512]{1,0:T(8,128)} async-done(((f32[1024,512]{1,0:T(8,128)}), f32[256,512]{1,0:T(8,128)}) %reduce-scatter.22.cloned.1.call-update) | async-done | bytes 524304 | tf_op jit(solution)/shard_map/reduce_scatter | solution.py:64
  815.8 3.3 fusion.8
  822.1 2.4 pad_maximum_fusion
  824.6 2.8 fusion.12
  827.4 73.4 %reduce-scatter.24.cloned.1.call-done = f32[256,2,512]{0,2,1:T(8,128)} async-done(((f32[1024,2,512]{0,2,1:T(8,128)}), f32[256,2,512]{0,2,1:T(8,128)}) %reduce-scatter.24.cloned.1.call-update) | async-done | bytes 1048592 | tf_op jit(solution)/shard_map/reduce_scatter | solution.py:254
  902.1 1.9 pad_maximum_fusion.1
  904.1 64.0 %all-gather.14.cloned.1.call-done = bf16[1024,1536]{0,1:T(8,128)(2,1)} async-done(((bf16[256,1536]{0,1:T(8,128)(2,1)}), bf16[1024,1536]{0,1:T(8,128)(2,1)}) %all-gather.14.cloned.1.call-update) | async-done | bytes 3145744 | tf_op jit(solution)/shard_map/all_gather | solution.py:75
  968.1 3.9 fusion.53
  972.3 4.9 fusion.55
  977.3 2.7 fusion.56
  981.2 2.1 fusion.57
  983.6 3.0 convert_reduce_fusion
  987.3 11.7 %all-reduce.5 = (f32[2,512]{1,0:T(2,128)}, f32[256]{0:T(256)}, f32[2048]{0:T(1024)}, f32[256]{0:T(256)}) all-reduce(f32[2,512]{1,0:T(2,128)S(1)} %pad_maximum_fusion.3, f32[256]{0:T(256)S(1)} %convert_reduce_fusion.3, f32[2048]{0:T(1024)S(1)} %convert_reduce_fusion, ...), channel_id=1, replica_groups=mesh['dp'=4,'row'=4,'col'=2] {'dp'}, use_global_device_ids=true, to_apply=%region_36.37 | all-reduce | flops 3584 | bytes 28672 | tf_op jit(solution)/shard_map/psum | solution.py:294
  1000.6 14.2 %all-reduce = (f32[256]{0:T(256)}, f32[256]{0:T(256)}, f32[256]{0:T(256)}, f32[256]{0:T(256)}) all-reduce(f32[256]{0:T(256)S(1)} %get-tuple-element.125, f32[256]{0:T(256)S(1)} %get-tuple-element.130, f32[256]{0:T(256)S(1)} %get-tuple-element.123, f32[256]{0:T(256)S(1)} %get-tuple-element.129), channel_id=1, replica_groups=mesh['dp'=4,'row'=4,'col'=2] {'dp','col'}, use_global_device_ids=true, to_apply=%region_31.32 | all-reduce | flops 1024 | bytes 8192 | tf_op jit(solution)/shard_map/psum | solution.py:313
  1014.8 8.9 all-reduce.1
  1023.7 2.2 fusion.24
  1025.9 88.7 %all-reduce.9.cloned.1.call-done = (f32[256,3,512]{0,2,1:T(8,128)}, f32[512,256]{1,0:T(8,128)}, f32[256,2048]{1,0:T(8,128)}, f32[2048,256]{1,0:T(8,128)}) async-done(((f32[256,3,512]{0,2,1:T(8,128)}, f32[512,256]{1,0:T(8,128)}, f32[256,2048]{1,0:T(8,128)}, f32[2048,256]{1,0:T(8,128)}), (f32[256,3,512]{0,2,1:T(8,128)}, f32[512,256]{1,0:T(8,128)}, f32[256,2048]{1,0:T(8,128)}, ...) | async-done | bytes 6291472 | tf_op jit(solution)/shard_map/psum | solution.py:294
  1114.6 3.2 copy.55
  (147 shorter events, 27.9 us)
Async XLA Ops:
  7.2 265.1 %copy-start = (bf16[256,2048]{1,0:T(8,128)(2,1)S(1)}, bf16[256,2048]{1,0:T(8,128)(2,1)}, u32[]{:S(2)}) copy-start(bf16[256,2048]{1,0:T(8,128)(2,1)} %param.28) | copy-start | bytes 3145732
  7.2 137.4 %reduce-scatter.10.cloned.1.call-start = ((), (), s32[]{:S(2)}) async-start(), calls=%async_computation.9 | async-start | bytes 7864320 | tf_op jit(solution)/shard_map/reduce_scatter | solution.py:64
  30.2 5.3 copy-start.9
  31.8 3.7 copy-start.13
  35.5 159.0 %all-gather.6.cloned.1.call-start = ((), (), s32[]{:S(2)}) async-start(), calls=%async_computation.10 | async-start | bytes 2621440 | tf_op jit(solution)/shard_map/all_gather | solution.py:225
  36.2 111.5 %copy-start.26 = (s32[1024]{0:T(1024)S(1)}, s32[1024]{0:T(1024)}, u32[]{:S(2)}) copy-start(s32[1024]{0:T(1024)} %param.19) | copy-start | bytes 12292
  36.2 111.7 %copy-start.35 = (s32[13]{0:T(128)S(1)}, s32[13]{0:T(128)}, u32[]{:S(2)}) copy-start(s32[13]{0:T(128)} %param.18) | copy-start | bytes 160
  146.7 49.7 %copy-start.19 = (f32[256,1,512]{0,2,1:T(8,128)}, f32[256,1,512]{0,2,1:T(8,128)S(1)}, u32[]{:S(2)}) copy-start(f32[256,1,512]{0,2,1:T(8,128)S(1)} %get-tuple-element.162) | copy-start | bytes 1572868
  147.6 82.1 %all-gather.8.cloned.1.call-start = ((), (), s32[]{:S(2)}) async-start(), calls=%async_computation.11 | async-start | bytes 1310720 | tf_op jit(solution)/shard_map/all_gather | solution.py:75
  194.5 1.9 copy-start.22
  196.3 1.8 copy-start.8
  198.1 2.9 copy-start.2
  199.2 30.5 %copy-start.24 = (bf16[512,256]{1,0:T(8,128)(2,1)S(1)}, bf16[512,256]{1,0:T(8,128)(2,1)}, u32[]{:S(2)}) copy-start(bf16[512,256]{1,0:T(8,128)(2,1)} %param.24) | copy-start | bytes 786436
  201.1 31.4 %copy-start.23 = (bf16[512,256]{1,0:T(8,128)(2,1)S(1)}, bf16[512,256]{1,0:T(8,128)(2,1)}, u32[]{:S(2)}) copy-start(bf16[512,256]{1,0:T(8,128)(2,1)} %param.17) | copy-start | bytes 786436
  201.1 51.3 %reduce-scatter.12.cloned.1.call-start = ((), (), s32[]{:S(2)}) async-start(), calls=%async_computation.12 | async-start | bytes 1572864 | tf_op jit(solution)/shard_map/reduce_scatter | solution.py:82
  232.4 166.1 %reduce-scatter.18.cloned.1.call-start = ((), (), s32[]{:S(2)}) async-start(), calls=%async_computation.16 | async-start | bytes 10485760 | tf_op jit(solution)/shard_map/reduce_scatter | solution.py:64
  249.4 3.0 copy-start.4
  249.4 3.0 copy-start.33
  249.4 14.9 %copy-start.27 = (f32[256]{0:T(256)S(1)}, f32[256]{0:T(256)}, u32[]{:S(2)}) copy-start(f32[256]{0:T(256)} %param.26) | copy-start | bytes 3076
  249.4 14.9 %copy-start.31 = (f32[256]{0:T(256)S(1)}, f32[256]{0:T(256)}, u32[]{:S(2)}) copy-start(f32[256]{0:T(256)} %param.27) | copy-start | bytes 3076
  249.4 296.6 %reduce-scatter.14.cloned.1.call-start = ((), (), s32[]{:S(2)}) async-start(), calls=%async_computation.13 | async-start | bytes 10485760 | tf_op jit(solution)/shard_map/reduce_scatter | solution.py:64
  276.8 269.2 %copy-start.29 = (f32[2048]{0:T(1024)S(1)}, f32[2048]{0:T(1024)}, u32[]{:S(2)}) copy-start(f32[2048]{0:T(1024)} %param.29) | copy-start | bytes 24580
  276.8 354.5 %all-gather.12.cloned.1.call-start = ((), (), s32[]{:S(2)}) async-start(), calls=%async_computation.17 | async-start | bytes 5242880 | tf_op jit(solution)/shard_map/all_gather | solution.py:75
  549.7 163.2 %all-gather.10.cloned.1.call-start = ((), (), s32[]{:S(2)}) async-start(), calls=%async_computation.14 | async-start | bytes 5242880 | tf_op jit(solution)/shard_map/all_gather | solution.py:75
  550.5 184.2 %reduce-scatter.20.cloned.1.call-start = ((), (), s32[]{:S(2)}) async-start(), calls=%async_computation.18 | async-start | bytes 1572864 | tf_op jit(solution)/shard_map/reduce_scatter | solution.py:82
  635.8 121.9 %copy-start.32 = (f32[256]{0:T(256)S(1)}, f32[256]{0:T(256)}, u32[]{:S(2)}) copy-start(f32[256]{0:T(256)} %param.31) | copy-start | bytes 3076
  635.8 121.9 %reduce-scatter.16.cloned.1.call-start = ((), (), s32[]{:S(2)}) async-start(), calls=%async_computation.15 | async-start | bytes 1572864 | tf_op jit(solution)/shard_map/reduce_scatter | solution.py:82
  717.6 97.0 %reduce-scatter.22.cloned.1.call-start = ((), (), s32[]{:S(2)}) async-start(), calls=%async_computation.19 | async-start | bytes 2621440 | tf_op jit(solution)/shard_map/reduce_scatter | solution.py:64
  770.6 130.2 %reduce-scatter.24.cloned.1.call-start = ((), (), s32[]{:S(2)}) async-start(), calls=%async_computation.20 | async-start | bytes 5242880 | tf_op jit(solution)/shard_map/reduce_scatter | solution.py:254
  815.8 3.5 copy-start.3
  820.6 1.0 copy-start.20
  824.6 143.5 %all-gather.14.cloned.1.call-start = ((), (), s32[]{:S(2)}) async-start(), calls=%async_computation.21 | async-start | bytes 3932160 | tf_op jit(solution)/shard_map/all_gather | solution.py:75
  827.4 140.7 %copy-start.14 = (bf16[256,3,512]{0,2,1:T(8,128)(2,1)S(1)}, bf16[256,3,512]{0,2,1:T(8,128)(2,1)}, u32[]{:S(2)}) copy-start(bf16[256,3,512]{0,2,1:T(8,128)(2,1)} %copy-done.13) | copy-start | bytes 2359300
  904.0 68.3 %copy-start.16 = (bf16[1024,256]{1,0:T(8,128)(2,1)S(1)}, bf16[1024,256]{1,0:T(8,128)(2,1)}, u32[]{:S(2)}) copy-start(bf16[1024,256]{1,0:T(8,128)(2,1)} %copy-done.15) | copy-start | bytes 1572868
  904.0 95.0 %reduce-scatter.26.cloned.1.call-start = ((), (), s32[]{:S(2)}) async-start(), calls=%async_computation.22 | async-start | bytes 1572864 | tf_op jit(solution)/shard_map/reduce_scatter | solution.py:82
  972.0 5.2 copy-start.6
  972.0 142.6 %all-reduce.9.cloned.1.call-start = ((), (), s32[]{:S(2)}) async-start(), calls=%async_computation.23 | async-start | bytes 12582912 | tf_op jit(solution)/shard_map/psum | solution.py:294
  972.3 4.9 copy-start.34
  977.3 2.7 copy-start.7
  977.3 4.0 copy-start.10
  977.3 4.0 copy-start.11
  983.4 3.4 copy-start.12
  983.6 15.4 %copy-start.28 = (f32[256]{0:T(256)S(1)}, f32[256]{0:T(256)}, u32[]{:S(2)}) copy-start(f32[256]{0:T(256)} %param.20) | copy-start | bytes 3076
  986.6 37.1 %copy-start.21 = (f32[512,256]{1,0:T(8,128)S(1)}, f32[512,256]{1,0:T(8,128)}, u32[]{:S(2)}) copy-start(f32[512,256]{1,0:T(8,128)} %get-tuple-element.156) | copy-start | bytes 1572868
  1114.6 3.2 copy-start.25
  1114.6 4.0 copy-start.18
  1117.8 2.1 copy-start.17
  1118.6 2.6 copy-start.1
  (3 other events, 2.3 us)
Sparse Core Ops, SparseCore 0:
  35.6 108.9 reduce-scatter.9
  147.7 46.7 all-gather.5
  201.2 28.4 all-gather.7
  232.5 19.8 reduce-scatter.11
  254.7 143.6 reduce-scatter.17
  400.8 145.1 reduce-scatter.13
  549.8 81.4 all-gather.11
  633.6 79.2 all-gather.9
  715.8 18.8 reduce-scatter.19
  737.3 20.3 reduce-scatter.15
  770.7 43.8 reduce-scatter.21
  824.7 76.0 reduce-scatter.23
  904.1 63.9 all-gather.13
  972.2 18.4 reduce-scatter.25
  994.3 120.2 all-reduce.8
where the time goes:
time: 1130 us
  waiting for transfers between devices  909 us (80%)
  blocking collectives  104 us (9%)
  matrix products  53.8 us (5%)
  other arithmetic  30.3 us (3%)
  local copies, waits for them, and re-layouts  15.1 us (1%)
  between operations  14.3 us (1%)
    reduce_scatter x4, waiting for transfers between devices, across_rows(): lax.psum_scatter(partial_term(jnp.int32(0), row_count * lax.axis_size('ro...  422 us
    all_gather x4, waiting for transfers between devices, across_cols(): gathered = lax.all_gather(operand, 'row', axis=0, tiled=True)  250 us
    psum x1, waiting for transfers between devices, on_device(): lax.psum((weight_terms[0], weight_terms[1], weight_terms[2], weight_terms...  88.7 us
    reduce_scatter x1, waiting for transfers between devices, on_device(): lax.psum_scatter(jnp.stack([key_grad.reshape(-1, col_width), value_grad.r...  73.4 us
    all_gather x1, waiting for transfers between devices, on_device(): lax.all_gather(jnp.stack([keys_here, values_here], axis=1), 'row', axis=0...  44.8 us
    psum x4, blocking collectives, width_sums(): lax.psum((jnp.sum(first_term, axis=1), jnp.sum(second_term, axis=1)), 'row')  44.6 us
    all_gather x4, blocking collectives, across_rows(): gathered = lax.all_gather(operand, 'col', axis=0, tiled=True)  33.2 us
    reduce_scatter x4, waiting for transfers between devices, across_cols(): lax.psum_scatter(partial_term(jnp.int32(0), row_count * lax.axis_size('co...  29.8 us
  transfers between devices with their start and end apart: 15, of which 14 were waited for; matrix products, arithmetic and copies ran while one was open for 4% of the time, Pallas kernels for 0%

commit v1 on v0

--- a/solution.py
+++ b/solution.py
@@ -222,9 +222,14 @@
     queries = (projected[:, 0] + b_qv[0]).astype(jnp.bfloat16)
     keys_here = projected[:, 1].astype(jnp.bfloat16)
     values_here = (projected[:, 2] + b_qv[1]).astype(jnp.bfloat16)
-    pair_all = lax.all_gather(
-        jnp.stack([keys_here, values_here], axis=1), "row", axis=0, tiled=True
-    )
+    x = jnp.stack([keys_here, values_here], axis=1)
+    ways, here, step = (lax.axis_size("row"), lax.axis_index("row"), x.shape[0])
+    shape = [n * ways if d == 0 else n for d, n in enumerate(x.shape)]
+    full = lax.dynamic_update_slice_in_dim(jnp.zeros(shape, x.dtype), x, here * step, axis=0)
+    for far in range(1, ways):
+        x = lax.ppermute(x, "row", [(d, (d + 1) % ways) for d in range(ways)])
+        full = lax.dynamic_update_slice_in_dim(full, x, (here - far) % ways * step, axis=0)
+    pair_all = full
     key_rows = pair_all[:, 0].reshape(-1, heads_here, HD)
     value_rows = pair_all[:, 1].reshape(-1, heads_here, HD)
     query_heads = queries.reshape(tok_rows, heads_here, HD)

time: 1130 us -> 1130 us (level)
    all_gather x1 -> x0, waiting for transfers between devices: 44.8 us -> none  [on_device(): lax.all_gather(jnp.stack([keys_here, values_here], axis=1), 'row', axis=0...]
    ppermute x0 -> x3, waiting for transfers between devices: none -> 39.9 us  [on_device(): x = lax.ppermute(x, 'row', [(d, (d + 1) % ways) for d in range(ways)])]
  transfers between devices with their start and end apart: 15 -> 17, of which waited for: 14 -> 16; matrix products, arithmetic and copies ran while one was open for 4% -> 4% of each run, Pallas kernels for 0% -> 0%
where the time goes in v1:
time: 1130 us
  waiting for transfers between devices  906 us (80%)
  blocking collectives  104 us (9%)
  matrix products  52.3 us (5%)
  other arithmetic  30.1 us (3%)
  local copies, waits for them, and re-layouts  17.3 us (2%)
  between operations  14.4 us (1%)
    reduce_scatter x4, waiting for transfers between devices, across_rows(): lax.psum_scatter(partial_term(jnp.int32(0), row_count * lax.axis_size('ro...  421 us
    all_gather x4, waiting for transfers between devices, across_cols(): gathered = lax.all_gather(operand, 'row', axis=0, tiled=True)  250 us
    psum x1, waiting for transfers between devices, on_device(): lax.psum((weight_terms[0], weight_terms[1], weight_terms[2], weight_terms...  88.7 us
    reduce_scatter x1, waiting for transfers between devices, on_device(): lax.psum_scatter(jnp.stack([key_grad.reshape(-1, col_width), value_grad.r...  73.4 us
    psum x4, blocking collectives, width_sums(): lax.psum((jnp.sum(first_term, axis=1), jnp.sum(second_term, axis=1)), 'row')  44.6 us
    ppermute x3, waiting for transfers between devices, on_device(): x = lax.ppermute(x, 'row', [(d, (d + 1) % ways) for d in range(ways)])  39.9 us
    all_gather x4, blocking collectives, across_rows(): gathered = lax.all_gather(operand, 'col', axis=0, tiled=True)  33.2 us
    reduce_scatter x4, waiting for transfers between devices, across_cols(): lax.psum_scatter(partial_term(jnp.int32(0), row_count * lax.axis_size('co...  31.5 us
  transfers between devices with their start and end apart: 17, of which 16 were waited for; matrix products, arithmetic and copies ran while one was open for 4% of the time, Pallas kernels for 0%

profile of v1, /device:TPU:0, one launch (start us, length us, event | category | flops | bytes accessed | tf_op | source)
XLA Modules:
  0.0 1126.6 jit_solution(4954430919635949657)
XLA Ops:
  8.5 13.5 %all-reduce.4 = (f32[512]{0:T(512)S(1)}, f32[512]{0:T(512)S(1)}) all-reduce(f32[512]{0:T(512)S(1)} %get-tuple-element.134, f32[512]{0:T(512)S(1)} %get-tuple-element.133), channel_id=1, replica_groups=mesh['dp'=4,'row'=4,'col'=2] {'row'}, use_global_device_ids=true, to_apply=%region_3.4 | all-reduce | flops 1024 | bytes 8192 | tf_op jit(solution)/shard_map/psum | solution.py:23
  23.1 7.0 all_gather.24
  31.8 3.7 fusion.46
  36.2 108.4 %reduce-scatter.10.cloned.1.call-done = f32[256,1536]{1,0:T(8,128)} async-done(((f32[1024,1536]{1,0:T(8,128)}), f32[256,1536]{1,0:T(8,128)}) %reduce-scatter.10.cloned.1.call-update) | async-done | bytes 1572880 | tf_op jit(solution)/shard_map/reduce_scatter | solution.py:64
  144.6 1.9 copy.51
  150.2 14.3 %collective-permute-done = bf16[256,2,512]{0,2,1:T(8,128)(2,1)} collective-permute-done((bf16[256,2,512]{0,2,1:T(8,128)(2,1)}, bf16[256,2,512]{0,2,1:T(8,128)(2,1)}, u32[]{:S(2)}, u32[]{:S(2)}) %collective-permute-start) | collective-permute-done | bytes 524320 | tf_op jit(solution)/shard_map/ppermute | solution.py:230
  165.3 14.2 %collective-permute-done.1 = bf16[256,2,512]{0,2,1:T(8,128)(2,1)} collective-permute-done((bf16[256,2,512]{0,2,1:T(8,128)(2,1)}, bf16[256,2,512]{0,2,1:T(8,128)(2,1)}, u32[]{:S(2)}, u32[]{:S(2)}) %collective-permute-start.1) | collective-permute-done | bytes 524320 | tf_op jit(solution)/shard_map/ppermute | solution.py:230
  181.9 11.5 %collective-permute-done.2 = bf16[256,2,512]{0,2,1:T(8,128)(2,1)} collective-permute-done((bf16[256,2,512]{0,2,1:T(8,128)(2,1)}, bf16[256,2,512]{0,2,1:T(8,128)(2,1)}, u32[]{:S(2)}, u32[]{:S(2)}) %collective-permute-start.2) | collective-permute-done | bytes 524320 | tf_op jit(solution)/shard_map/ppermute | solution.py:230
  197.6 1.9 fusion.13
  199.6 28.5 %all-gather.5.cloned.1.call-done = bf16[1024,512]{0,1:T(8,128)(2,1)} async-done(((bf16[256,512]{0,1:T(8,128)(2,1)}), bf16[1024,512]{0,1:T(8,128)(2,1)}) %all-gather.5.cloned.1.call-update) | async-done | bytes 1048592 | tf_op jit(solution)/shard_map/all_gather | solution.py:75
  228.0 2.7 fusion.47
  230.8 10.4 all_gather.28
  242.0 4.5 fusion.50
  246.6 4.2 reduce-scatter.12.cloned.1.call-done
  252.0 10.6 all-reduce.3
  262.8 7.0 all_gather.26
  270.7 4.5 fusion.48
  275.4 121.4 %reduce-scatter.18.cloned.1.call-done = f32[256,2048]{1,0:T(8,128)} async-done(((f32[1024,2048]{1,0:T(8,128)}), f32[256,2048]{1,0:T(8,128)}) %reduce-scatter.18.cloned.1.call-update) | async-done | bytes 2097168 | tf_op jit(solution)/shard_map/reduce_scatter | solution.py:64
  396.8 147.5 %reduce-scatter.14.cloned.1.call-done = f32[256,2048]{1,0:T(8,128)} async-done(((f32[1024,2048]{1,0:T(8,128)}), f32[256,2048]{1,0:T(8,128)}) %reduce-scatter.14.cloned.1.call-update) | async-done | bytes 2097168 | tf_op jit(solution)/shard_map/reduce_scatter | solution.py:64
  544.4 3.7 fusion.7
  548.9 80.8 %all-gather.9.cloned.1.call-done = bf16[1024,2048]{1,0:T(8,128)(2,1)} async-done(((bf16[256,2048]{1,0:T(8,128)(2,1)}), bf16[1024,2048]{1,0:T(8,128)(2,1)}) %all-gather.9.cloned.1.call-update) | async-done | bytes 4194320 | tf_op jit(solution)/shard_map/all_gather | solution.py:75
  629.7 4.4 fusion.51
  634.2 77.0 %all-gather.7.cloned.1.call-done = bf16[1024,2048]{1,0:T(8,128)(2,1)} async-done(((bf16[256,2048]{1,0:T(8,128)(2,1)}), bf16[1024,2048]{1,0:T(8,128)(2,1)}) %all-gather.7.cloned.1.call-update) | async-done | bytes 4194320 | tf_op jit(solution)/shard_map/all_gather | solution.py:75
  711.2 4.4 fusion.49
  715.7 17.3 %reduce-scatter.20.cloned.1.call-done = f32[512,256]{1,0:T(8,128)} async-done(((f32[1024,256]{1,0:T(8,128)}), f32[512,256]{1,0:T(8,128)}) %reduce-scatter.20.cloned.1.call-update) | async-done | bytes 524304 | tf_op jit(solution)/shard_map/reduce_scatter | solution.py:82
  734.4 11.7 %all-reduce.2 = (f32[512]{0:T(512)S(1)}, f32[512]{0:T(512)S(1)}) all-reduce(f32[512]{0:T(512)S(1)} %get-tuple-element.124, f32[512]{0:T(512)S(1)} %get-tuple-element.128), channel_id=1, replica_groups=mesh['dp'=4,'row'=4,'col'=2] {'row'}, use_global_device_ids=true, to_apply=%region_21.22 | all-reduce | flops 1024 | bytes 8192 | tf_op jit(solution)/shard_map/psum | solution.py:23
  746.1 10.1 reduce-scatter.16.cloned.1.call-done
  756.2 2.4 fusion.39
  758.6 8.7 all_gather.30
  767.3 1.8 fusion.52
  769.2 44.0 %reduce-scatter.22.cloned.1.call-done = f32[256,512]{1,0:T(8,128)} async-done(((f32[1024,512]{1,0:T(8,128)}), f32[256,512]{1,0:T(8,128)}) %reduce-scatter.22.cloned.1.call-update) | async-done | bytes 524304 | tf_op jit(solution)/shard_map/reduce_scatter | solution.py:64
  814.4 3.2 fusion.8
  821.0 2.4 pad_maximum_fusion
  823.4 2.8 fusion.12
  826.2 73.4 %reduce-scatter.24.cloned.1.call-done = f32[256,2,512]{0,2,1:T(8,128)} async-done(((f32[1024,2,512]{0,2,1:T(8,128)}), f32[256,2,512]{0,2,1:T(8,128)}) %reduce-scatter.24.cloned.1.call-update) | async-done | bytes 1048592 | tf_op jit(solution)/shard_map/reduce_scatter | solution.py:259
  900.9 1.9 pad_maximum_fusion.1
  902.9 64.0 %all-gather.11.cloned.1.call-done = bf16[1024,1536]{0,1:T(8,128)(2,1)} async-done(((bf16[256,1536]{0,1:T(8,128)(2,1)}), bf16[1024,1536]{0,1:T(8,128)(2,1)}) %all-gather.11.cloned.1.call-update) | async-done | bytes 3145744 | tf_op jit(solution)/shard_map/all_gather | solution.py:75
  966.9 3.9 fusion.53
  971.2 4.9 fusion.55
  976.1 2.7 fusion.56
  980.0 2.1 fusion.57
  982.4 3.0 convert_reduce_fusion
  986.1 11.7 %all-reduce.5 = (f32[2,512]{1,0:T(2,128)}, f32[256]{0:T(256)}, f32[2048]{0:T(1024)}, f32[256]{0:T(256)}) all-reduce(f32[2,512]{1,0:T(2,128)S(1)} %pad_maximum_fusion.3, f32[256]{0:T(256)S(1)} %convert_reduce_fusion.3, f32[2048]{0:T(1024)S(1)} %convert_reduce_fusion, ...), channel_id=1, replica_groups=mesh['dp'=4,'row'=4,'col'=2] {'dp'}, use_global_device_ids=true, to_apply=%region_36.37 | all-reduce | flops 3584 | bytes 28672 | tf_op jit(solution)/shard_map/psum | solution.py:299
  999.4 14.2 %all-reduce = (f32[256]{0:T(256)}, f32[256]{0:T(256)}, f32[256]{0:T(256)}, f32[256]{0:T(256)}) all-reduce(f32[256]{0:T(256)S(1)} %get-tuple-element.125, f32[256]{0:T(256)S(1)} %get-tuple-element.130, f32[256]{0:T(256)S(1)} %get-tuple-element.123, f32[256]{0:T(256)S(1)} %get-tuple-element.129), channel_id=1, replica_groups=mesh['dp'=4,'row'=4,'col'=2] {'dp','col'}, use_global_device_ids=true, to_apply=%region_31.32 | all-reduce | flops 1024 | bytes 8192 | tf_op jit(solution)/shard_map/psum | solution.py:318
  1013.6 8.9 all-reduce.1
  1022.5 2.2 fusion.24
  1024.7 88.7 %all-reduce.9.cloned.1.call-done = (f32[256,3,512]{0,2,1:T(8,128)}, f32[512,256]{1,0:T(8,128)}, f32[256,2048]{1,0:T(8,128)}, f32[2048,256]{1,0:T(8,128)}) async-done(((f32[256,3,512]{0,2,1:T(8,128)}, f32[512,256]{1,0:T(8,128)}, f32[256,2048]{1,0:T(8,128)}, f32[2048,256]{1,0:T(8,128)}), (f32[256,3,512]{0,2,1:T(8,128)}, f32[512,256]{1,0:T(8,128)}, f32[256,2048]{1,0:T(8,128)}, ...) | async-done | bytes 6291472 | tf_op jit(solution)/shard_map/psum | solution.py:299
  1113.4 3.2 copy.58
  (158 shorter events, 35.0 us)
Async XLA Ops:
  7.2 263.5 %copy-start = (bf16[256,2048]{1,0:T(8,128)(2,1)S(1)}, bf16[256,2048]{1,0:T(8,128)(2,1)}, u32[]{:S(2)}) copy-start(bf16[256,2048]{1,0:T(8,128)(2,1)} %param.28) | copy-start | bytes 3145732
  7.2 137.4 %reduce-scatter.10.cloned.1.call-start = ((), (), s32[]{:S(2)}) async-start(), calls=%async_computation.9 | async-start | bytes 7864320 | tf_op jit(solution)/shard_map/reduce_scatter | solution.py:64
  30.2 5.3 copy-start.11
  31.8 3.7 copy-start.15
  35.5 192.5 %all-gather.5.cloned.1.call-start = ((), (), s32[]{:S(2)}) async-start(), calls=%async_computation.10 | async-start | bytes 1310720 | tf_op jit(solution)/shard_map/all_gather | solution.py:75
  146.5 3.6 copy-start.28
  146.5 3.7 copy-start.37
  148.6 15.8 %collective-permute-start = (bf16[256,2,512]{0,2,1:T(8,128)(2,1)}, bf16[256,2,512]{0,2,1:T(8,128)(2,1)}, u32[]{:S(2)}, u32[]{:S(2)}) collective-permute-start(bf16[256,2,512]{0,2,1:T(8,128)(2,1)} %get-tuple-element.165), channel_id=1, source_target_pairs={{0,2},{2,4},{4,6},{6,0},{1,3},{3,5},{5,7},{7,1},{8,10},{10,12},{12... | collective-permute-start | bytes 1572872 | tf_op jit(solution)/shard_map/ppermute | solution.py:230
  164.4 15.0 %collective-permute-start.1 = (bf16[256,2,512]{0,2,1:T(8,128)(2,1)}, bf16[256,2,512]{0,2,1:T(8,128)(2,1)}, u32[]{:S(2)}, u32[]{:S(2)}) collective-permute-start(bf16[256,2,512]{0,2,1:T(8,128)(2,1)} %collective-permute-done), channel_id=1, source_target_pairs={{0,2},{2,4},{4,6},{6,0},{1,3},{3,5},{5,7},{7,1},{8,10},{10,12},{12... | collective-permute-start | bytes 1572872 | tf_op jit(solution)/shard_map/ppermute | solution.py:230
  179.4 14.1 %collective-permute-start.2 = (bf16[256,2,512]{0,2,1:T(8,128)(2,1)}, bf16[256,2,512]{0,2,1:T(8,128)(2,1)}, u32[]{:S(2)}, u32[]{:S(2)}) collective-permute-start(bf16[256,2,512]{0,2,1:T(8,128)(2,1)} %collective-permute-done.1), channel_id=1, source_target_pairs={{0,2},{2,4},{4,6},{6,0},{1,3},{3,5},{5,7},{7,1},{8,10},{10,12},{12... | collective-permute-start | bytes 1572872 | tf_op jit(solution)/shard_map/ppermute | solution.py:230
  180.7 14.0 %copy-start.21 = (f32[256,1,512]{0,2,1:T(8,128)S(1)}, f32[256,1,512]{0,2,1:T(8,128)}, u32[]{:S(2)}) copy-start(f32[256,1,512]{0,2,1:T(8,128)} %get-tuple-element.162) | copy-start | bytes 1572868
  194.8 2.8 copy-start.9
  196.5 2.9 copy-start.2
  197.6 30.4 %copy-start.26 = (bf16[512,256]{1,0:T(8,128)(2,1)S(1)}, bf16[512,256]{1,0:T(8,128)(2,1)}, u32[]{:S(2)}) copy-start(bf16[512,256]{1,0:T(8,128)(2,1)} %param.24) | copy-start | bytes 786436
  199.5 31.3 %copy-start.25 = (bf16[512,256]{1,0:T(8,128)(2,1)S(1)}, bf16[512,256]{1,0:T(8,128)(2,1)}, u32[]{:S(2)}) copy-start(bf16[512,256]{1,0:T(8,128)(2,1)} %param.17) | copy-start | bytes 786436
  199.5 42.5 %copy-start.24 = (bf16[2048,256]{1,0:T(8,128)(2,1)S(1)}, bf16[2048,256]{1,0:T(8,128)(2,1)}, u32[]{:S(2)}) copy-start(bf16[2048,256]{1,0:T(8,128)(2,1)} %param.30) | copy-start | bytes 3145732
  199.5 51.3 %reduce-scatter.12.cloned.1.call-start = ((), (), s32[]{:S(2)}) async-start(), calls=%async_computation.11 | async-start | bytes 1572864 | tf_op jit(solution)/shard_map/reduce_scatter | solution.py:82
  230.7 166.1 %reduce-scatter.18.cloned.1.call-start = ((), (), s32[]{:S(2)}) async-start(), calls=%async_computation.15 | async-start | bytes 10485760 | tf_op jit(solution)/shard_map/reduce_scatter | solution.py:64
  246.5 4.3 copy-start.4
  246.5 4.3 copy-start.35
  246.5 16.1 %copy-start.29 = (f32[256]{0:T(256)S(1)}, f32[256]{0:T(256)}, u32[]{:S(2)}) copy-start(f32[256]{0:T(256)} %param.26) | copy-start | bytes 3076
  246.5 16.1 %copy-start.33 = (f32[256]{0:T(256)S(1)}, f32[256]{0:T(256)}, u32[]{:S(2)}) copy-start(f32[256]{0:T(256)} %param.27) | copy-start | bytes 3076
  246.5 297.8 %reduce-scatter.14.cloned.1.call-start = ((), (), s32[]{:S(2)}) async-start(), calls=%async_computation.12 | async-start | bytes 10485760 | tf_op jit(solution)/shard_map/reduce_scatter | solution.py:64
  275.2 269.2 %copy-start.31 = (f32[2048]{0:T(1024)S(1)}, f32[2048]{0:T(1024)}, u32[]{:S(2)}) copy-start(f32[2048]{0:T(1024)} %param.29) | copy-start | bytes 24580
  275.2 354.5 %all-gather.9.cloned.1.call-start = ((), (), s32[]{:S(2)}) async-start(), calls=%async_computation.16 | async-start | bytes 5242880 | tf_op jit(solution)/shard_map/all_gather | solution.py:75
  548.1 163.2 %all-gather.7.cloned.1.call-start = ((), (), s32[]{:S(2)}) async-start(), calls=%async_computation.13 | async-start | bytes 5242880 | tf_op jit(solution)/shard_map/all_gather | solution.py:75
  548.8 184.2 %reduce-scatter.20.cloned.1.call-start = ((), (), s32[]{:S(2)}) async-start(), calls=%async_computation.17 | async-start | bytes 1572864 | tf_op jit(solution)/shard_map/reduce_scatter | solution.py:82
  634.2 122.0 %copy-start.34 = (f32[256]{0:T(256)S(1)}, f32[256]{0:T(256)}, u32[]{:S(2)}) copy-start(f32[256]{0:T(256)} %param.31) | copy-start | bytes 3076
  634.2 122.0 %reduce-scatter.16.cloned.1.call-start = ((), (), s32[]{:S(2)}) async-start(), calls=%async_computation.14 | async-start | bytes 1572864 | tf_op jit(solution)/shard_map/reduce_scatter | solution.py:82
  715.7 97.4 %reduce-scatter.22.cloned.1.call-start = ((), (), s32[]{:S(2)}) async-start(), calls=%async_computation.18 | async-start | bytes 2621440 | tf_op jit(solution)/shard_map/reduce_scatter | solution.py:64
  769.1 130.5 %reduce-scatter.24.cloned.1.call-start = ((), (), s32[]{:S(2)}) async-start(), calls=%async_computation.19 | async-start | bytes 5242880 | tf_op jit(solution)/shard_map/reduce_scatter | solution.py:259
  814.3 3.5 copy-start.3
  814.4 3.7 copy-start.10
  823.4 143.5 %all-gather.11.cloned.1.call-start = ((), (), s32[]{:S(2)}) async-start(), calls=%async_computation.20 | async-start | bytes 3932160 | tf_op jit(solution)/shard_map/all_gather | solution.py:75
  826.2 140.7 %copy-start.16 = (bf16[256,3,512]{0,2,1:T(8,128)(2,1)S(1)}, bf16[256,3,512]{0,2,1:T(8,128)(2,1)}, u32[]{:S(2)}) copy-start(bf16[256,3,512]{0,2,1:T(8,128)(2,1)} %copy-done.15) | copy-start | bytes 2359300
  902.8 68.3 %copy-start.18 = (bf16[1024,256]{1,0:T(8,128)(2,1)S(1)}, bf16[1024,256]{1,0:T(8,128)(2,1)}, u32[]{:S(2)}) copy-start(bf16[1024,256]{1,0:T(8,128)(2,1)} %copy-done.17) | copy-start | bytes 1572868
  902.9 94.9 %reduce-scatter.26.cloned.1.call-start = ((), (), s32[]{:S(2)}) async-start(), calls=%async_computation.21 | async-start | bytes 1572864 | tf_op jit(solution)/shard_map/reduce_scatter | solution.py:82
  970.9 5.2 copy-start.6
  970.9 142.6 %all-reduce.9.cloned.1.call-start = ((), (), s32[]{:S(2)}) async-start(), calls=%async_computation.22 | async-start | bytes 12582912 | tf_op jit(solution)/shard_map/psum | solution.py:299
  971.1 4.9 copy-start.36
  976.1 2.7 copy-start.7
  976.1 4.0 copy-start.12
  976.1 3.9 copy-start.13
  982.2 3.4 copy-start.14
  982.4 15.4 %copy-start.30 = (f32[256]{0:T(256)S(1)}, f32[256]{0:T(256)}, u32[]{:S(2)}) copy-start(f32[256]{0:T(256)} %param.20) | copy-start | bytes 3076
  985.4 37.1 %copy-start.23 = (f32[512,256]{1,0:T(8,128)S(1)}, f32[512,256]{1,0:T(8,128)}, u32[]{:S(2)}) copy-start(f32[512,256]{1,0:T(8,128)} %get-tuple-element.156) | copy-start | bytes 1572868
  1113.4 3.2 copy-start.27
  1113.4 4.0 copy-start.20
  (7 other events, 9.9 us)
Sparse Core Ops, SparseCore 0:
  35.6 108.9 reduce-scatter.9
  199.6 28.3 all-gather.4
  230.8 19.8 reduce-scatter.11
  253.1 143.6 reduce-scatter.17
  399.1 145.1 reduce-scatter.13
  548.2 81.4 all-gather.8
  631.9 79.2 all-gather.6
  714.1 18.8 reduce-scatter.19
  735.8 20.3 reduce-scatter.15
  769.2 43.8 reduce-scatter.21
  823.5 76.0 reduce-scatter.23
  903.0 63.9 all-gather.10
  971.0 18.4 reduce-scatter.25
  993.1 120.2 all-reduce.8
